TPU v7x, 256 devices: a whole 4x4x8 slice. The times are simulated.
256 devices in a mesh: pb: 16 (over x, z_hi), sa: 16 (over z_lo, y, core).
Axes of the slice: x: 4, y: 4, z: 8 (z_hi: 4, z_lo: 2; z = z_hi * 2 + z_lo), core: 2. Of those that a mesh axis runs over, the one named last changes fastest.
Arguments:
- question_states: bfloat16 [16, 16, 256, 768], P('pb', 'sa'), may hold values from -16 to 16
- question_ids: int32 [16, 16, 256], P('pb'), may hold values from 0 to 30521, as said below
- q_inner_weight: bfloat16 [768, 3072], P(None, 'sa'), may hold values from -0.21875 to 0.21875
- q_outer_weight: bfloat16 [3072, 768], P('sa'), may hold values from -0.109375 to 0.109375
- q_norm_gain: float32 [768], replicated, may hold values from 0.1 to 1.9
- sql_states: bfloat16 [16, 16, 256, 768], P('sa', 'pb'), may hold values from -16 to 16
- sql_ids: int32 [16, 16, 256], P('sa'), may hold values from 0 to 32099, as said below
- s_inner_weight: bfloat16 [768, 3072], P(None, 'pb'), may hold values from -0.21875 to 0.21875
- s_outer_weight: bfloat16 [3072, 768], P('pb'), may hold values from -0.109375 to 0.109375
- s_norm_gain: float32 [768], replicated, may hold values from 0.1 to 1.9
- positive_column: int32 [256], P('pb'), may hold values from 0 to 255, each once
Outputs:
- loss: float32 [], replicated
- q_inner_grad: float32 [768, 3072], P(None, 'sa')
- q_outer_grad: float32 [3072, 768], P('sa')
- q_gain_grad: float32 [768], replicated
- s_inner_grad: float32 [768, 3072], P(None, 'pb')
- s_outer_grad: float32 [3072, 768], P('pb')
- s_gain_grad: float32 [768], replicated
Inputs may be any that keep to these rules, and one draw needn't show every extreme that they name: `question_ids`: each sequence is a run of nonzero ids followed by padding zeros, the run 3 * 64 long or longer. `sql_ids`: each sequence is a run of nonzero ids followed by padding zeros, the run 3 * 64 long or longer.
All inputs are finite; a program needn't handle non-finite values.
Results may differ from a plain program's by a relative error of at most 0.0051.
Values may be sent and summed in bfloat16 or wider, within the bound.
A program may use at most 128 MiB of HBM per device.

v0:
```python
import math
import jax
import jax.numpy as jnp
from jax import lax
from jax.sharding import PartitionSpec as P

D = 768
HIGH = lax.Precision.HIGHEST


def apply_rms_norm(input_float, norm_gain_vector, root_mean_square):
    if root_mean_square:
        input_normalized = input_float * lax.rsqrt(
            jnp.mean(input_float * input_float, axis=-1, keepdims=True) + 1e-06
        )
    else:
        mean_removed = input_float - jnp.mean(input_float, axis=-1, keepdims=True)
        input_normalized = mean_removed * lax.rsqrt(
            jnp.mean(mean_removed * mean_removed, axis=-1, keepdims=True) + 1e-05
        )
    return (input_normalized, (input_normalized * norm_gain_vector).astype(jnp.bfloat16))


def gelu_value(v):
    return 0.5 * v * (1.0 + lax.erf(v / math.sqrt(2.0)))


def gelu_slope(v):
    return 0.5 * (1.0 + lax.erf(v / math.sqrt(2.0))) + v * jnp.exp(-0.5 * v * v) / math.sqrt(
        2.0 * math.pi
    )


def pool_weights(ids):
    mask = (ids > 0).astype(jnp.float32)
    return mask / jnp.sum(mask, axis=-1, keepdims=True)


def forward_block(states, ids, inner, norm_gain_vector, root_mean_square):
    count, length, width = states.shape
    input_float = states.astype(jnp.float32).reshape(count * length, width)
    input_normalized, normalized_rows = apply_rms_norm(
        input_float, norm_gain_vector, root_mean_square
    )
    pre = jnp.dot(normalized_rows, inner, preferred_element_type=jnp.float32)
    hidden = gelu_value(pre).reshape(count, length, -1)
    return jnp.einsum("nt,ntf->nf", pool_weights(ids), hidden, precision=HIGH)


def residual_pool(states, ids):
    return jnp.einsum("nt,ntd->nd", pool_weights(ids), states.astype(jnp.float32), precision=HIGH)


def backward_block(states, ids, inner, norm_gain_vector, root_mean_square, hidden_grad):
    count, length, width = states.shape
    input_float = states.astype(jnp.float32).reshape(count * length, width)
    input_normalized, normalized_rows = apply_rms_norm(
        input_float, norm_gain_vector, root_mean_square
    )
    pre = jnp.dot(normalized_rows, inner, preferred_element_type=jnp.float32)
    weights = pool_weights(ids)
    slope = gelu_slope(pre).reshape(count, length, -1)
    dpre = (
        (weights[:, :, None] * hidden_grad[:, None, :] * slope)
        .reshape(count * length, -1)
        .astype(jnp.bfloat16)
    )
    inner_layer_grad = lax.dot_general(
        normalized_rows, dpre, (((0,), (0,)), ((), ())), preferred_element_type=jnp.float32
    )
    normalized_grad = lax.dot_general(
        dpre, inner, (((1,), (1,)), ((), ())), preferred_element_type=jnp.float32
    )
    return (inner_layer_grad, jnp.sum(input_normalized * normalized_grad, axis=0))


def per_device(
    question_states,
    question_ids,
    q_inner_weight,
    q_outer_weight,
    q_norm_gain,
    sql_states,
    sql_ids,
    s_inner_weight,
    s_outer_weight,
    s_norm_gain,
    positive_column,
):
    scale = 1.0 / math.sqrt(D)
    q_table = question_ids[0]
    s_table = sql_ids[0]
    q_rows = q_table.shape[0]
    s_rows = s_table.shape[0]
    own_count = question_states.shape[1]
    q_place = lax.axis_index("sa")
    s_place = lax.axis_index("pb")

    def s_forward(piece):
        pooled = forward_block(piece[0], s_table, s_inner_weight, s_norm_gain, True)
        return pooled

    ids = q_table
    pooled = forward_block(
        lax.all_gather(question_states, "sa", axis=1, tiled=True)[0],
        ids,
        q_inner_weight,
        q_norm_gain,
        False,
    )
    s_pooled = s_forward(lax.all_gather(sql_states, "pb", axis=1, tiled=True))
    q_first = q_place * own_count
    s_first = s_place * own_count
    q_own = residual_pool(
        question_states[0], lax.dynamic_slice_in_dim(q_table, q_first, own_count, 0)
    )
    s_own = residual_pool(sql_states[0], lax.dynamic_slice_in_dim(s_table, s_first, own_count, 0))
    q_resid = lax.dynamic_update_slice_in_dim(
        jnp.zeros((q_rows, D), jnp.float32), q_own, q_first, 0
    )
    s_resid = lax.dynamic_update_slice_in_dim(
        jnp.zeros((s_rows, D), jnp.float32), s_own, s_first, 0
    )
    q_outer_f = q_outer_weight.astype(jnp.float32)
    s_outer_f = s_outer_weight.astype(jnp.float32)
    q_embed = lax.psum(jnp.dot(pooled, q_outer_f, precision=HIGH) + q_resid, "sa")
    s_embed = lax.psum(jnp.dot(s_pooled, s_outer_f, precision=HIGH) + s_resid, "pb")
    tile = scale * lax.dot_general(q_embed, s_embed, (((1,), (1,)), ((), ())), precision=HIGH)
    columns = q_place * s_rows + jnp.arange(s_rows, dtype=jnp.int32)
    match = (positive_column[:, None] == columns[None, :]).astype(jnp.float32)
    row_top = lax.pmax(jnp.max(tile, axis=1), "sa")
    row_total, row_pos = lax.psum(
        (jnp.sum(jnp.exp(tile - row_top[:, None]), axis=1), jnp.sum(match * tile, axis=1)), "sa"
    )
    col_top = lax.pmax(jnp.max(tile, axis=0), "pb")
    col_total, col_pos = lax.psum(
        (jnp.sum(jnp.exp(tile - col_top[None, :]), axis=0), jnp.sum(match * tile, axis=0)), "pb"
    )
    row_lse = row_top + jnp.log(row_total)
    col_lse = col_top + jnp.log(col_total)
    pairs = q_rows * lax.axis_size("pb")
    row_part = jnp.where(q_place == 0, jnp.sum(row_lse - row_pos), 0.0)
    col_part = jnp.where(s_place == 0, jnp.sum(col_lse - col_pos), 0.0)
    loss_part = (row_part + col_part) / (2.0 * pairs)
    dscore = 0.5 * (
        jnp.exp(tile - row_lse[:, None]) + jnp.exp(tile - col_lse[None, :]) - 2.0 * match
    )
    q_grad = lax.psum(scale * jnp.dot(dscore, s_embed, precision=HIGH), "sa")
    s_grad = lax.psum(
        scale * lax.dot_general(dscore, q_embed, (((0,), (0,)), ((), ())), precision=HIGH), "pb"
    )
    q_outer_part = lax.dot_general(pooled, q_grad, (((0,), (0,)), ((), ())), precision=HIGH)
    s_outer_part = lax.dot_general(s_pooled, s_grad, (((0,), (0,)), ((), ())), precision=HIGH)
    q_hidden_grad = lax.dot_general(q_grad, q_outer_f, (((1,), (1,)), ((), ())), precision=HIGH)
    s_hidden_grad = lax.dot_general(s_grad, s_outer_f, (((1,), (1,)), ((), ())), precision=HIGH)

    def s_backward(piece):
        inner_layer_grad, gain_grad = backward_block(
            piece[0], s_table, s_inner_weight, s_norm_gain, True, s_hidden_grad
        )
        return (inner_layer_grad, gain_grad)

    ids = q_table
    inner_layer_grad, gain_grad = backward_block(
        lax.all_gather(question_states, "sa", axis=1, tiled=True)[0],
        ids,
        q_inner_weight,
        q_norm_gain,
        False,
        q_hidden_grad,
    )
    s_inner_part, s_gain_part = s_backward(lax.all_gather(sql_states, "pb", axis=1, tiled=True))
    q_inner_grad, q_outer_grad = lax.psum((inner_layer_grad, q_outer_part), "pb")
    s_inner_grad, s_outer_grad = lax.psum((s_inner_part, s_outer_part), "sa")
    q_gain_grad, s_gain_grad, loss = lax.psum((gain_grad, s_gain_part, loss_part), ("pb", "sa"))
    return (loss, q_inner_grad, q_outer_grad, q_gain_grad, s_inner_grad, s_outer_grad, s_gain_grad)


def solution(mesh):
    placed = (
        P("pb", "sa", None, None),
        P("pb", None, None),
        P(None, "sa"),
        P("sa", None),
        P(),
        P("sa", "pb", None, None),
        P("sa", None, None),
        P(None, "pb"),
        P("pb", None),
        P(),
        P("pb"),
    )
    return jax.shard_map(
        per_device,
        mesh=mesh,
        in_specs=placed,
        out_specs=(P(), P(None, "sa"), P("sa", None), P(), P(None, "pb"), P("pb", None), P()),
        check_vma=False,
    )
```

profile of v0, /device:TPU:1, one launch (start us, length us, event | category | flops | bytes accessed | tf_op | source)
XLA Modules:
  0.0 849.9 jit_solution(1982385561405561287)
XLA Ops:
  15.7 43.4 %all-gather.3.cloned.1.call-done = bf16[1,16,256,768]{3,2,0,1:T(8,128)(2,1)} async-done(((bf16[1,1,256,768]{3,2,0,1:T(8,128)(2,1)}), bf16[1,16,256,768]{3,2,0,1:T(8,128)(2,1)}) %all-gather.3.cloned.1.call-update) | async-done | bytes 6291472 | tf_op jit(solution)/shard_map/all_gather | solution.py:105
  59.1 3.8 convert_reduce_fusion
  63.7 1.9 multiply_reduce_fusion.3
  65.7 2.2 multiply_convert_fusion.1
  67.9 2.5 multiply_multiply_fusion.3
  70.5 2.7 fusion.16
  74.9 56.9 %psum.105 = f32[16,768]{1,0:T(8,128)S(1)} all-reduce(f32[16,768]{1,0:T(8,128)S(1)} %add.105), channel_id=1, replica_groups=mesh['pb'=16,'sa'=16] {'sa'}, use_global_device_ids=true, to_apply=%region_4.0 | all-reduce | flops 12288 | bytes 98304 | tf_op jit(solution)/shard_map/psum | solution.py:126
  131.7 27.8 %all-gather.5.cloned.1.call-done = bf16[1,16,256,768]{3,2,0,1:T(8,128)(2,1)} async-done(((bf16[1,1,256,768]{3,2,0,1:T(8,128)(2,1)}), bf16[1,16,256,768]{3,2,0,1:T(8,128)(2,1)}) %all-gather.5.cloned.1.call-update) | async-done | bytes 6291472 | tf_op jit(solution)/shard_map/all_gather | solution.py:111
  159.5 4.2 multiply_reduce_fusion.2
  165.9 3.6 multiply_multiply_fusion.2
  169.6 2.7 fusion.13
  174.8 67.6 %psum.106 = f32[16,768]{1,0:T(8,128)} all-reduce(f32[16,768]{1,0:T(8,128)S(1)} %add.109), channel_id=1, replica_groups=mesh['pb'=16,'sa'=16] {'pb'}, use_global_device_ids=true, to_apply=%region_8.0 | all-reduce | flops 12288 | bytes 98304 | tf_op jit(solution)/shard_map/psum | solution.py:127
  243.6 41.3 %pmax.14 = f32[16]{0:T(128)S(1)} all-reduce(f32[16]{0:T(128)S(1)} %get-tuple-element.12), channel_id=1, replica_groups=mesh['pb'=16,'sa'=16] {'sa'}, use_global_device_ids=true, to_apply=%region_10.0 | all-reduce | flops 16 | bytes 128 | tf_op jit(solution)/shard_map/pmax | solution.py:131
  284.9 32.1 %pmax.15 = f32[16]{0:T(128)S(1)} all-reduce(f32[16]{0:T(128)S(1)} %get-tuple-element.11), channel_id=1, replica_groups=mesh['pb'=16,'sa'=16] {'pb'}, use_global_device_ids=true, to_apply=%region_17.0 | all-reduce | flops 16 | bytes 128 | tf_op jit(solution)/shard_map/pmax | solution.py:135
  318.3 34.1 %psum.107 = f32[16]{0:T(128)S(1)} all-reduce(f32[16]{0:T(128)S(1)} %get-tuple-element.10), channel_id=1, replica_groups=mesh['pb'=16,'sa'=16] {'sa'}, use_global_device_ids=true, to_apply=%region_12.0 | all-reduce | flops 16 | bytes 128 | tf_op jit(solution)/shard_map/psum | solution.py:132
  352.4 34.7 %psum.109 = f32[16]{0:T(128)S(1)} all-reduce(f32[16]{0:T(128)S(1)} %get-tuple-element.9), channel_id=1, replica_groups=mesh['pb'=16,'sa'=16] {'pb'}, use_global_device_ids=true, to_apply=%region_19.0 | all-reduce | flops 16 | bytes 128 | tf_op jit(solution)/shard_map/psum | solution.py:136
  390.5 56.9 %all-reduce.1 = (f32[16]{0:T(128)}, f32[16,768]{1,0:T(8,128)S(1)}) all-reduce(f32[16]{0:T(128)} %get-tuple-element.8, f32[16,768]{1,0:T(8,128)} %convolution_multiply_fusion.1), channel_id=1, replica_groups=mesh['pb'=16,'sa'=16] {'sa'}, use_global_device_ids=true, to_apply=%region_14.0 | all-reduce | flops 12304 | bytes 98432 | tf_op jit(solution)/shard_map/psum | solution.py:132
  448.7 2.2 fusion.29
  451.4 4.4 copy.39
  455.8 63.2 %all-reduce.3 = (f32[16]{0:T(128)}, f32[16,768]{1,0:T(8,128)S(1)}) all-reduce(f32[16]{0:T(128)} %get-tuple-element.7, f32[16,768]{1,0:T(8,128)S(1)} %copy-done.27), channel_id=1, replica_groups=mesh['pb'=16,'sa'=16] {'pb'}, use_global_device_ids=true, to_apply=%region_21.0 | all-reduce | flops 12304 | bytes 98432 | tf_op jit(solution)/shard_map/psum | solution.py:136
  520.8 4.5 copy.42
  527.9 2.2 fusion.65
  530.3 2.8 fusion.12
  534.6 5.0 fusion.66
  539.8 5.9 multiply_reduce_fusion
  548.2 4.8 multiply_reduce_fusion.1
  553.1 89.9 %all-reduce = (f32[]{:T(128)}, f32[768]{0:T(1024)}, f32[768]{0:T(1024)}) all-reduce(f32[]{:T(128)S(6)} %div.107, f32[768]{0:T(1024)S(1)} %multiply_reduce_fusion.1, f32[768]{0:T(1024)S(1)} %multiply_reduce_fusion), channel_id=1, replica_groups=mesh['pb'=16,'sa'=16] {'pb','sa'}, use_global_device_ids=true, to_apply=%region_23.24 | all-reduce | flops 1537 | bytes 12296 | tf_op jit(solution)/shard_map/psum | solution.py:175
  643.0 57.8 %all-reduce.10.cloned.1.call-done = (f32[768,192]{0,1:T(8,128)}, f32[192,768]{1,0:T(8,128)}) async-done(((f32[768,192]{0,1:T(8,128)}, f32[192,768]{1,0:T(8,128)}), (f32[768,192]{0,1:T(8,128)}, f32[192,768]{1,0:T(8,128)})) %all-reduce.10.cloned.1.call-update) | async-done | bytes 1179664 | tf_op jit(solution)/shard_map/psum | solution.py:173
  700.8 135.9 %all-reduce.8.cloned.1.call-done = (f32[768,192]{0,1:T(8,128)}, f32[192,768]{1,0:T(8,128)}) async-done(((f32[768,192]{0,1:T(8,128)}, f32[192,768]{1,0:T(8,128)}), (f32[768,192]{0,1:T(8,128)}, f32[192,768]{1,0:T(8,128)})) %all-reduce.8.cloned.1.call-update) | async-done | bytes 1179664 | tf_op jit(solution)/shard_map/psum | solution.py:174
  836.7 2.0 copy.77
  838.7 1.9 copy.78
  840.6 1.9 copy.79
  (127 shorter events, 30.0 us)
Async XLA Ops:
  7.2 158.7 %copy-start = (bf16[768,192]{0,1:T(8,128)(2,1)S(1)}, bf16[768,192]{0,1:T(8,128)(2,1)}, u32[]{:S(2)}) copy-start(bf16[768,192]{0,1:T(8,128)(2,1)} %param.18) | copy-start | bytes 884740
  7.2 51.9 %all-gather.3.cloned.1.call-start = ((), (), s32[]{:S(2)}) async-start(), calls=%async_computation | async-start | bytes 6684672 | tf_op jit(solution)/shard_map/all_gather | solution.py:105
  7.9 151.6 %all-gather.5.cloned.1.call-start = ((), (), s32[]{:S(2)}) async-start(), calls=%async_computation.1 | async-start | bytes 6684672 | tf_op jit(solution)/shard_map/all_gather | solution.py:111
  8.7 692.1 %all-reduce.10.cloned.1.call-start = ((), (), s32[]{:S(2)}) async-start(), calls=%async_computation.3 | async-start | bytes 2359296 | tf_op jit(solution)/shard_map/psum | solution.py:173
  59.1 4.6 copy-start.1
  67.9 2.6 copy-start.2
  70.5 2.7 copy-start.12
  70.5 3.3 copy-start.7
  131.7 32.7 %copy-start.29 = (f32[768]{0:T(1024)S(1)}, f32[768]{0:T(1024)}, u32[]{:S(2)}) copy-start(f32[768]{0:T(1024)} %param.20) | copy-start | bytes 9220
  159.5 4.9 copy-start.4
  165.9 3.7 copy-start.3
  165.9 3.7 copy-start.20
  169.6 2.7 copy-start.13
  169.6 2.9 copy-start.8
  352.4 38.1 %copy-start.34 = (f32[16]{0:T(128)}, f32[16]{0:T(128)S(1)}, u32[]{:S(2)}) copy-start(f32[16]{0:T(128)S(1)} %log_add_fusion.1) | copy-start | bytes 196
  387.1 3.3 copy-start.32
  451.4 4.4 copy-start.27
  520.7 4.6 copy-start.6
  520.7 4.6 copy-start.19
  520.8 7.1 slice-start
  525.3 2.6 slice-start.1
  530.2 306.5 %all-reduce.8.cloned.1.call-start = ((), (), s32[]{:S(2)}) async-start(), calls=%async_computation.2 | async-start | bytes 2359296 | tf_op jit(solution)/shard_map/psum | solution.py:174
  534.6 5.1 copy-start.26
  539.7 6.0 copy-start.30
  539.7 6.0 copy-start.35
  539.7 7.2 copy-start.31
  539.7 7.2 copy-start.33
  539.7 8.5 copy-start.10
  539.7 8.5 copy-start.16
  539.7 8.5 copy-start.22
  539.7 8.5 copy-start.24
  836.7 5.8 copy-start.14
  (10 other events, 17.2 us)
Sparse Core Ops, SparseCore 0:
  9.9 49.1 all-gather.2
  61.5 97.9 all-gather.4
  530.3 170.4 all-reduce.9
  703.9 132.7 all-reduce.7
where the time goes:
time: 851 us; the launch traced here: 850 us
  blocking collectives  477 us (56%)
  waiting for transfers between devices  266 us (31%)
  matrix products  43.3 us (5%)
  other arithmetic  26 us (3%)
  local copies, waits for them, and re-layouts  20.5 us (2%)
  between operations  17 us (2%)
    psum x1, waiting for transfers between devices, per_device(): s_inner_grad, s_outer_grad = lax.psum((s_inner_part, s_outer_part), 'sa')  136 us
    psum x2, blocking collectives, per_device(): lax.psum((jnp.sum(jnp.exp(tile - col_top[None, :]), axis=0), jnp.sum(matc...  97.9 us
    psum x2, blocking collectives, per_device(): lax.psum((jnp.sum(jnp.exp(tile - row_top[:, None]), axis=1), jnp.sum(matc...  91 us
    psum x1, blocking collectives, per_device(): lax.psum((gain_grad, s_gain_part, loss_part), ('pb', 'sa'))  89.9 us
    psum x1, blocking collectives, per_device(): lax.psum(jnp.dot(s_pooled, s_outer_f, precision=HIGH) + s_resid, 'pb')  67.6 us
    psum x1, waiting for transfers between devices, per_device(): lax.psum((inner_layer_grad, q_outer_part), 'pb')  57.8 us
    psum x1, blocking collectives, per_device(): lax.psum(jnp.dot(pooled, q_outer_f, precision=HIGH) + q_resid, 'sa')  56.9 us
    all_gather x1, waiting for transfers between devices, per_device(): lax.all_gather(question_states, 'sa', axis=1, tiled=True)[0]  43.4 us
  transfers between devices with their start and end apart: 4, of which 4 were waited for; matrix products, arithmetic and copies ran while one was open for 5% of the time, Pallas kernels for 0%

commit v1 on v0

--- a/solution.py
+++ b/solution.py
@@ -108,7 +108,11 @@
         q_norm_gain,
         False,
     )
-    s_pooled = s_forward(lax.all_gather(sql_states, "pb", axis=1, tiled=True))
+    s_pooled = s_forward(
+        jnp.concatenate(
+            lax.all_to_all(jnp.stack([sql_states] * lax.axis_size("pb")), "pb", 0, 0), axis=1
+        )
+    )
     q_first = q_place * own_count
     s_first = s_place * own_count
     q_own = residual_pool(

time: 851 us -> 1050 us (1.23)
  waiting for transfers between devices: 266 us -> 433 us
  starting transfers between devices: 0.16 us -> 12.2 us
    all_gather x1, waiting for transfers between devices: 27.8 us -> 196 us  [per_device(): lax.all_gather(sql_states, 'pb', axis=1, tiled=True)]
    all_to_all x0 -> x1, starting transfers between devices: none -> 11.8 us  [per_device(): lax.all_to_all(jnp.stack([sql_states] * lax.axis_size('pb')), 'pb', 0, 0)]
  transfers between devices with their start and end apart: 4 -> 5, of which waited for: 4 -> 4; matrix products, arithmetic and copies ran while one was open for 5% -> 4% of each run, Pallas kernels for 0% -> 0%
where the time goes in v1:
time: 1050 us; the launch traced here: 1040 us
  blocking collectives  475 us (45%)
  waiting for transfers between devices  433 us (41%)
  matrix products  47.7 us (5%)
  other arithmetic  34 us (3%)
  local copies, waits for them, and re-layouts  24.4 us (2%)
  between operations  17.1 us (2%)
  starting transfers between devices  12.2 us (1%)
    all_gather x1, waiting for transfers between devices, per_device(): lax.all_gather(sql_states, 'pb', axis=1, tiled=True)  196 us
    psum x1, waiting for transfers between devices, per_device(): s_inner_grad, s_outer_grad = lax.psum((s_inner_part, s_outer_part), 'sa')  136 us
    psum x2, blocking collectives, per_device(): lax.psum((jnp.sum(jnp.exp(tile - col_top[None, :]), axis=0), jnp.sum(matc...  99 us
    psum x1, blocking collectives, per_device(): lax.psum((gain_grad, s_gain_part, loss_part), ('pb', 'sa'))  90.2 us
    psum x2, blocking collectives, per_device(): lax.psum((jnp.sum(jnp.exp(tile - row_top[:, None]), axis=1), jnp.sum(matc...  84.1 us
    psum x1, blocking collectives, per_device(): lax.psum(jnp.dot(s_pooled, s_outer_f, precision=HIGH) + s_resid, 'pb')  68.8 us
    psum x1, blocking collectives, per_device(): lax.psum(jnp.dot(pooled, q_outer_f, precision=HIGH) + q_resid, 'sa')  63.3 us
    psum x1, waiting for transfers between devices, per_device(): lax.psum((inner_layer_grad, q_outer_part), 'pb')  55.8 us
  transfers between devices with their start and end apart: 5, of which 4 were waited for; matrix products, arithmetic and copies ran while one was open for 4% of the time, Pallas kernels for 0%

profile of v1, /device:TPU:1, one launch (start us, length us, event | category | flops | bytes accessed | tf_op | source)
XLA Modules:
  0.0 1044.0 jit_solution(594147175180576336)
XLA Ops:
  8.7 4.2 stack.2
  12.9 11.8 %all-to-all-start = ((bf16[16,1,1,256,768]{4,3,2,1,0:T(8,128)(2,1)}), bf16[16,1,1,256,768]{4,3,2,1,0:T(8,128)(2,1)}, u32[]{:S(2)}, u32[]{:S(2)}) async-start(bf16[16,1,1,256,768]{4,3,2,1,0:T(8,128)(2,1)} %stack.2), calls=%async_computation | async-start | bytes 12582912 | tf_op jit(solution)/shard_map/all_to_all | solution.py:113
  28.9 195.6 %all-gather.5.cloned.1.call-done = bf16[1,16,256,768]{3,2,0,1:T(8,128)(2,1)} async-done(((bf16[1,1,256,768]{3,2,0,1:T(8,128)(2,1)}), bf16[1,16,256,768]{3,2,0,1:T(8,128)(2,1)}) %all-gather.5.cloned.1.call-update) | async-done | bytes 6291472 | tf_op jit(solution)/shard_map/all_gather | solution.py:176
  224.5 4.1 multiply_reduce_fusion.1
  228.6 44.5 %all-gather.3.cloned.1.call-done = bf16[1,16,256,768]{3,2,0,1:T(8,128)(2,1)} async-done(((bf16[1,1,256,768]{3,2,0,1:T(8,128)(2,1)}), bf16[1,16,256,768]{3,2,0,1:T(8,128)(2,1)}) %all-gather.3.cloned.1.call-update) | async-done | bytes 6291472 | tf_op jit(solution)/shard_map/all_gather | solution.py:105
  273.1 3.8 convert_reduce_fusion
  279.7 4.1 multiply_reduce_fusion.3
  283.9 8.6 multiply_convert_fusion
  292.5 2.4 add_multiply_fusion
  294.9 2.7 fusion.15
  298.2 68.8 %psum.106 = f32[16,768]{1,0:T(8,128)S(1)} all-reduce(f32[16,768]{1,0:T(8,128)S(1)} %add.119), channel_id=1, replica_groups=mesh['pb'=16,'sa'=16] {'pb'}, use_global_device_ids=true, to_apply=%region_8.0 | all-reduce | flops 12288 | bytes 98304 | tf_op jit(solution)/shard_map/psum | solution.py:131
  367.1 4.6 multiply_convert_fusion.1
  371.7 2.5 multiply_multiply_fusion.2
  374.3 2.7 fusion.18
  379.9 63.3 %psum.105 = f32[16,768]{1,0:T(8,128)} all-reduce(f32[16,768]{1,0:T(8,128)S(1)} %add.115), channel_id=1, replica_groups=mesh['pb'=16,'sa'=16] {'sa'}, use_global_device_ids=true, to_apply=%region_4.0 | all-reduce | flops 12288 | bytes 98304 | tf_op jit(solution)/shard_map/psum | solution.py:130
  444.3 32.1 %pmax.15 = f32[16]{0:T(128)S(1)} all-reduce(f32[16]{0:T(128)S(1)} %get-tuple-element.11), channel_id=1, replica_groups=mesh['pb'=16,'sa'=16] {'pb'}, use_global_device_ids=true, to_apply=%region_17.0 | all-reduce | flops 16 | bytes 128 | tf_op jit(solution)/shard_map/pmax | solution.py:139
  476.5 37.8 %pmax.14 = f32[16]{0:T(128)S(1)} all-reduce(f32[16]{0:T(128)S(1)} %get-tuple-element.12), channel_id=1, replica_groups=mesh['pb'=16,'sa'=16] {'sa'}, use_global_device_ids=true, to_apply=%region_10.0 | all-reduce | flops 16 | bytes 128 | tf_op jit(solution)/shard_map/pmax | solution.py:135
  515.7 34.7 %psum.109 = f32[16]{0:T(128)S(1)} all-reduce(f32[16]{0:T(128)S(1)} %get-tuple-element.9), channel_id=1, replica_groups=mesh['pb'=16,'sa'=16] {'pb'}, use_global_device_ids=true, to_apply=%region_19.0 | all-reduce | flops 16 | bytes 128 | tf_op jit(solution)/shard_map/psum | solution.py:140
  550.4 34.4 %psum.107 = f32[16]{0:T(128)S(1)} all-reduce(f32[16]{0:T(128)S(1)} %get-tuple-element.10), channel_id=1, replica_groups=mesh['pb'=16,'sa'=16] {'sa'}, use_global_device_ids=true, to_apply=%region_12.0 | all-reduce | flops 16 | bytes 128 | tf_op jit(solution)/shard_map/psum | solution.py:136
  588.1 49.7 %all-reduce.1 = (f32[16]{0:T(128)}, f32[16,768]{1,0:T(8,128)S(1)}) all-reduce(f32[16]{0:T(128)} %get-tuple-element.8, f32[16,768]{1,0:T(8,128)} %convolution_multiply_fusion.1), channel_id=1, replica_groups=mesh['pb'=16,'sa'=16] {'sa'}, use_global_device_ids=true, to_apply=%region_14.0 | all-reduce | flops 12304 | bytes 98432 | tf_op jit(solution)/shard_map/psum | solution.py:136
  642.0 64.2 %all-reduce.3 = (f32[16]{0:T(128)}, f32[16,768]{1,0:T(8,128)}) all-reduce(f32[16]{0:T(128)} %get-tuple-element.7, f32[16,768]{1,0:T(8,128)} %convolution_multiply_fusion), channel_id=1, replica_groups=mesh['pb'=16,'sa'=16] {'pb'}, use_global_device_ids=true, to_apply=%region_21.0 | all-reduce | flops 12304 | bytes 98432 | tf_op jit(solution)/shard_map/psum | solution.py:140
  707.6 2.3 fusion.26
  711.3 2.7 copy.39
  716.7 2.2 fusion.67
  719.5 4.4 copy.42
  724.2 7.7 fusion.14
  733.1 2.2 fusion.68
  735.5 5.9 multiply_reduce_fusion
  743.9 4.9 multiply_reduce_fusion.2
  748.8 90.2 %all-reduce = (f32[]{:T(128)}, f32[768]{0:T(1024)}, f32[768]{0:T(1024)}) all-reduce(f32[]{:T(128)S(6)} %div.111, f32[768]{0:T(1024)S(1)} %multiply_reduce_fusion.2, f32[768]{0:T(1024)S(1)} %multiply_reduce_fusion), channel_id=1, replica_groups=mesh['pb'=16,'sa'=16] {'pb','sa'}, use_global_device_ids=true, to_apply=%region_23.24 | all-reduce | flops 1537 | bytes 12296 | tf_op jit(solution)/shard_map/psum | solution.py:179
  839.0 55.8 %all-reduce.10.cloned.1.call-done = (f32[768,192]{0,1:T(8,128)}, f32[192,768]{1,0:T(8,128)}) async-done(((f32[768,192]{0,1:T(8,128)}, f32[192,768]{1,0:T(8,128)}), (f32[768,192]{0,1:T(8,128)}, f32[192,768]{1,0:T(8,128)})) %all-reduce.10.cloned.1.call-update) | async-done | bytes 1179664 | tf_op jit(solution)/shard_map/psum | solution.py:177
  894.8 136.0 %all-reduce.8.cloned.1.call-done = (f32[768,192]{0,1:T(8,128)}, f32[192,768]{1,0:T(8,128)}) async-done(((f32[768,192]{0,1:T(8,128)}, f32[192,768]{1,0:T(8,128)}), (f32[768,192]{0,1:T(8,128)}, f32[192,768]{1,0:T(8,128)})) %all-reduce.8.cloned.1.call-update) | async-done | bytes 1179664 | tf_op jit(solution)/shard_map/psum | solution.py:178
  (130 shorter events, 35.9 us)
Async XLA Ops:
  7.2 285.3 %copy-start = (bf16[768,192]{0,1:T(8,128)(2,1)S(1)}, bf16[768,192]{0,1:T(8,128)(2,1)}, u32[]{:S(2)}) copy-start(bf16[768,192]{0,1:T(8,128)(2,1)} %param.18) | copy-start | bytes 884740
  7.2 217.3 %all-gather.5.cloned.1.call-start = ((), (), s32[]{:S(2)}) async-start(), calls=%async_computation.2 | async-start | bytes 6684672 | tf_op jit(solution)/shard_map/all_gather | solution.py:176
  7.9 265.2 %all-gather.3.cloned.1.call-start = ((), (), s32[]{:S(2)}) async-start(), calls=%async_computation.1 | async-start | bytes 6684672 | tf_op jit(solution)/shard_map/all_gather | solution.py:105
  12.9 11.8 %copy-start.20 = (s32[1,16,256]{2,1,0:T(8,128)S(1)}, s32[1,16,256]{2,1,0:T(8,128)}, u32[]{:S(2)}) copy-start(s32[1,16,256]{2,1,0:T(8,128)} %param.17) | copy-start | bytes 49156
  12.9 11.8 %copy-start.21 = (s32[1,16,256]{2,1,0:T(8,128)S(1)}, s32[1,16,256]{2,1,0:T(8,128)}, u32[]{:S(2)}) copy-start(s32[1,16,256]{2,1,0:T(8,128)} %param.12) | copy-start | bytes 49156
  12.9 266.8 %all-to-all-start = ((bf16[16,1,1,256,768]{4,3,2,1,0:T(8,128)(2,1)}), bf16[16,1,1,256,768]{4,3,2,1,0:T(8,128)(2,1)}, u32[]{:S(2)}, u32[]{:S(2)}) async-start(bf16[16,1,1,256,768]{4,3,2,1,0:T(8,128)(2,1)} %stack.2), calls=%async_computation | async-start | bytes 12582912 | tf_op jit(solution)/shard_map/all_to_all | solution.py:113
  24.7 870.2 %all-reduce.10.cloned.1.call-start = ((), (), s32[]{:S(2)}) async-start(), calls=%async_computation.4 | async-start | bytes 2359296 | tf_op jit(solution)/shard_map/psum | solution.py:177
  228.6 55.2 %copy-start.18 = (f32[2,2,8,128]{3,1,2,0:T(2,128)}, f32[2,2,8,128]{3,1,2,0:T(2,128)S(1)}, u32[]{:S(2)}) copy-start(f32[2,2,8,128]{3,1,2,0:T(2,128)S(1)} %copy.43) | copy-start | bytes 49156
  273.1 4.6 copy-start.1
  277.0 90.1 %copy-start.14 = (f32[2,2,8,128]{3,1,2,0:T(2,128)}, f32[2,2,8,128]{3,1,2,0:T(2,128)S(1)}, u32[]{:S(2)}) copy-start(f32[2,2,8,128]{3,1,2,0:T(2,128)S(1)} %copy.34) | copy-start | bytes 49156
  279.7 87.4 %copy-start.16 = (f32[2,2,8,128]{3,1,2,0:T(2,128)}, f32[2,2,8,128]{3,1,2,0:T(2,128)S(1)}, u32[]{:S(2)}) copy-start(f32[2,2,8,128]{3,1,2,0:T(2,128)S(1)} %copy.35) | copy-start | bytes 49156
  279.7 4.2 copy-start.24
  294.9 3.0 copy-start.3
  294.9 72.1 %copy-start.23 = (f32[768]{0:T(1024)S(1)}, f32[768]{0:T(1024)}, u32[]{:S(2)}) copy-start(f32[768]{0:T(1024)} %param.15) | copy-start | bytes 9220
  367.1 4.6 copy-start.10
  374.3 3.3 copy-start.4
  550.4 37.7 %copy-start.27 = (f32[16]{0:T(128)}, f32[16]{0:T(128)S(1)}, u32[]{:S(2)}) copy-start(f32[16]{0:T(128)S(1)} %log_add_fusion) | copy-start | bytes 196
  584.8 3.3 copy-start.29
  711.3 5.5 slice-start
  719.4 4.8 copy-start.22
  723.9 9.3 slice-start.2
  723.9 306.9 %all-reduce.8.cloned.1.call-start = ((), (), s32[]{:S(2)}) async-start(), calls=%async_computation.3 | async-start | bytes 2359296 | tf_op jit(solution)/shard_map/psum | solution.py:178
  724.2 8.9 slice-start.3
  735.4 6.0 copy-start.25
  735.4 6.0 copy-start.30
  735.4 7.2 copy-start.26
  735.4 7.2 copy-start.28
  735.4 8.5 copy-start.6
  735.4 8.5 copy-start.11
  735.4 8.5 copy-start.15
  735.4 8.5 copy-start.17
  1030.8 5.8 copy-start.9
  (9 other events, 18.7 us)
Sparse Core Ops, SparseCore 0:
  10.5 213.9 all-gather.4
  226.3 46.7 all-gather.2
  724.0 170.7 all-reduce.9
  897.9 132.8 all-reduce.7
